TPU v7x, 32 devices: a whole 2x2x4 slice. The times are simulated.
32 devices in a mesh: prow: 8 (over z, x), pcol: 4 (over y, core).
Axes of the slice: x: 2, y: 2, z: 4, core: 2. Of those that a mesh axis runs over, the one named last changes fastest.
Arguments:
- matrix: float32 [24, 512, 6, 2048], P(None, 'prow', None, 'pcol'), may hold values from -6 to 6
- pivots: int32 [2, 512], replicated, may hold values from 0 to 12287, as said below
- lower_inv: float32 [2, 512, 512], replicated
- upper_inv: float32 [2, 512, 512], replicated
Outputs:
- factored: float32 [24, 512, 6, 2048], P(None, 'prow', None, 'pcol')
Inputs may be any that keep to these rules, and one draw needn't show every extreme that they name: pivots[k, i] is at least k * 512 + i; every panel has one entry equal to 12287, and the first panel's first row keeps its place.
All inputs are finite; a program needn't handle non-finite values.
Results may differ from a plain program's by a relative error of at most 0.00011.
Values sent between devices are 32-bit elements; how exact they have to be, the bound alone decides.
No kernel may reach another device: no remote copies, remote signals or barrier semaphores. Data moves between devices by JAX's collectives and lax.ppermute only.
A program may use at most 128 MiB of HBM per device.

v0:
```python
import functools
import math

import jax
import jax.numpy as jnp
from jax import lax
from jax.experimental.layout import Layout, with_layout_constraint
from jax.experimental import pallas as pl
from jax.experimental.pallas import tpu as pltpu
from jax.sharding import PartitionSpec as P


def div_by(value, count):
    if count & (count - 1) == 0:
        return lax.shift_right_logical(value, jnp.full_like(value, count.bit_length() - 1))
    return lax.div(value, jnp.full_like(value, count))


def mod_by(value, count):
    if count & (count - 1) == 0:
        return value & (count - 1)
    return value - div_by(value, count) * count


def ring_place(index, count):
    return jnp.where(index % 2 == 0, index // 2, count - 1 - index // 2)


def split(value):
    high = value.astype(jnp.bfloat16)
    return high, (value - high.astype(jnp.float32)).astype(jnp.bfloat16)


def dot3(left_high, left_low, right_high, right_low):
    def one(left, right):
        return jnp.dot(left, right, preferred_element_type=jnp.float32)

    return one(left_high, right_high) + (one(left_high, right_low) + one(left_low, right_high))


def turned(row):
    return jnp.transpose(jnp.broadcast_to(row, (8, row.shape[1])))[:, :1]


def routing_kernel(
    me_ref,
    piv_row,
    piv_col,
    send_ref,
    place_ref,
    column_ref,
    out_ref,
    row_ref,
    slot_ref,
    count_ref,
    over_ref,
    want_ref,
    from_ref,
    *,
    sizes,
):
    panel, part, devices, cap, pair_cap, _, rows = sizes
    total = piv_row.shape[1]
    me = me_ref[0]
    p_row = piv_row[...]
    p_col = piv_col[...]
    lane = lax.broadcasted_iota(jnp.int32, (1, total), 1)
    sub = lax.broadcasted_iota(jnp.int32, (total, 1), 0)

    def top(mask, value):
        return jnp.max(jnp.where(mask, value, -1), axis=0, keepdims=True)

    def pick(index_row, value_col):
        return jnp.sum(jnp.where(sub == index_row, value_col, 0), axis=0, keepdims=True)

    chain = top((p_col == lane) & (sub < lane), sub)
    start = jnp.where(chain >= 0, chain, lane)

    def step(carry):
        pointer, _ = carry
        further = pick(pointer, turned(pointer))
        return further, jnp.max(jnp.abs(further - pointer))

    before, _ = lax.while_loop(lambda carry: carry[1] > 0, step, (start, jnp.int32(1)))
    same = p_col == p_row
    last = top(same & (sub < lane), sub)
    final = top(same, sub)
    wanted = jnp.where(last >= 0, pick(last, turned(before)), p_row)

    def owner(row):
        return div_by(mod_by(row, panel), part)

    def spot(row):
        return div_by(row, panel) * part + mod_by(row, part)

    holder = owner(wanted)
    rank = jnp.sum(jnp.where((turned(holder) == holder) & (sub < lane), 1, 0), axis=0, keepdims=True)
    moved = (final == lane) & (p_row >= total)
    source = owner(before)
    target = owner(p_row)
    pair = jnp.where(moved, source * devices + target, -1)
    pair_rank = jnp.sum(jnp.where((turned(pair) == pair) & (sub < lane), 1, 0), axis=0, keepdims=True)
    distance = ring_place(me, devices) - ring_place(holder, devices)
    distance = jnp.where(distance < 0, distance + devices, distance)
    place = distance * cap + rank
    place_ref[...] = place
    column_ref[...] = turned(place)

    def table(width, code, value):
        slots = lax.broadcasted_iota(jnp.int32, (1, width), 1)
        return jnp.sum(jnp.where(turned(code) == slots, turned(value), 0), axis=0, keepdims=True)

    send_ref[...] = table(send_ref.shape[1], jnp.where((holder == me) & (rank < cap), rank, -1), spot(wanted))
    want_ref[...] = wanted
    from_ref[...] = jnp.where(moved, before, -1)
    fits = moved & (pair_rank < pair_cap)
    going = fits & (source == me)
    coming = fits & (target == me)
    out_ref[...] = table(out_ref.shape[1], jnp.where(going, target * pair_cap + pair_rank, -1), spot(before))
    band = jnp.where(coming, div_by(spot(p_row), rows), -1)
    band_rank = jnp.sum(jnp.where((turned(band) == band) & (sub < lane), 1, 0), axis=0, keepdims=True)
    code = jnp.where(coming, band * (devices * pair_cap) + band_rank, -1)
    row_ref[...] = table(row_ref.shape[1], code, mod_by(spot(p_row), rows))
    slot_ref[...] = table(slot_ref.shape[1], code, source * pair_cap + pair_rank)
    kinds = lax.broadcasted_iota(jnp.int32, (1, count_ref.shape[1]), 1)
    count_ref[...] = jnp.sum(jnp.where(turned(band) == kinds, 1, 0), axis=0, keepdims=True)
    excess = jnp.maximum(jnp.max(rank) - cap, jnp.max(jnp.where(moved, pair_rank, 0)) - pair_cap)
    over_ref[...] = jnp.full(over_ref.shape, excess, jnp.int32)


def plain(value):
    return with_layout_constraint(value, Layout(major_to_minor=tuple(range(value.ndim))))


def lanes(count):
    return -(-count // 128) * 128


def routing(me, pivots, sizes):
    _, _, devices, cap, pair_cap, bands, _ = sizes
    total = pivots.size
    pairs = devices * pair_cap
    shapes = [lanes(cap), total, 0, lanes(pairs), lanes(bands * pairs), lanes(bands * pairs), 128, 128, total, total]
    return pl.pallas_call(
        functools.partial(routing_kernel, sizes=sizes),
        out_shape=[jax.ShapeDtypeStruct((1, width) if width else (total, 1), jnp.int32) for width in shapes],
        in_specs=[
            pl.BlockSpec(memory_space=pltpu.SMEM),
            pl.BlockSpec(memory_space=pltpu.VMEM),
            pl.BlockSpec(memory_space=pltpu.VMEM),
        ],
        name="routing",
    )(me, pivots.reshape(1, total), pivots.reshape(total, 1))


def move_rows(count, unroll, load, store):
    def body(step, _):
        rows = [step * unroll + inner for inner in range(unroll)]
        values = [load(row) for row in rows]
        for row, value in zip(rows, values):
            store(row, value)
        return 0

    lax.fori_loop(0, count // unroll, body, 0)


def pack_kernel(at_ref, x_ref, o_ref, *, part):
    def load(row):
        spot = at_ref[row]
        return x_ref[spot // part, 0, pl.ds(spot % part, 1), :]

    def store(row, value):
        o_ref[0, pl.ds(row, 1), :] = value

    move_rows(o_ref.shape[1], 8, load, store)


def pack(at, x, col, per, cap):
    blocks, _, part, width = x.shape
    return pl.pallas_call(
        functools.partial(pack_kernel, part=part),
        grid_spec=pltpu.PrefetchScalarGridSpec(
            num_scalar_prefetch=1,
            grid=(per,),
            in_specs=[pl.BlockSpec((blocks, 1, part, width), lambda i, at: (0, col + i, 0, 0))],
            out_specs=pl.BlockSpec((1, cap, width), lambda i, at: (i, 0, 0)),
        ),
        out_shape=jax.ShapeDtypeStruct((per, cap, width), jnp.float32),
        cost_estimate=pl.CostEstimate(flops=0, transcendentals=0, bytes_accessed=3 * per * blocks * part * width * 4),
        name="pack",
    )(at, x)


def piece_specs(pieces, offset):
    def spec(piece, start):
        count = piece.shape[0]
        return pl.BlockSpec((1,) + piece.shape[1:], lambda i, *_: (jnp.clip(i - start, 0, count - 1), 0, 0))

    per = pieces[0].shape[0]
    left, right = pieces[-2:]
    later = offset if left.shape[0] == per else offset + left.shape[0]
    return [spec(piece, offset) for piece in pieces[:-1]] + [spec(right, later)]


def load_pieces(pieces, cap, width, index, half, store):
    count = len(pieces) - 1
    far = (count + 1) // 2
    for place in range(count - 1):
        store((place if place < far else place + 1) * cap, 0, pieces[place][0])
    left, right = pieces[-2:]
    if left.shape[2] < width:
        store(far * cap, 0, left[0])
        store(far * cap, left.shape[2], right[0])
    else:
        store(far * cap, 0, jnp.where(index < half, left[0], right[0]))


def unpack_kernel(flag_ref, at_ref, *refs, cap):
    pieces, o_ref, sent_ref, buffer = refs[:-3], refs[-3], refs[-2], refs[-1]

    def put(row, col, value):
        buffer[row : row + value.shape[0], col : col + value.shape[1]] = value

    load_pieces(pieces, cap, buffer.shape[1], 0, 1, put)

    def load(row):
        return buffer[pl.ds(at_ref[row], 1), :]

    def store(row, value):
        o_ref[pl.ds(row, 1), :] = value

    move_rows(o_ref.shape[0], 8, load, store)
    panel = sent_ref.shape[0]
    sent_ref[...] = jnp.where(flag_ref[2] == 0, o_ref[panel:], o_ref[:panel])


def unpack(flags, at, pieces, cap, devices, panel):
    total = at.shape[0]
    _, _, width = pieces[0].shape
    return pl.pallas_call(
        functools.partial(unpack_kernel, cap=cap),
        grid_spec=pltpu.PrefetchScalarGridSpec(
            num_scalar_prefetch=2,
            grid=(1,),
            in_specs=piece_specs(pieces, 0),
            out_specs=[
                pl.BlockSpec((total, width), lambda i, *_: (0, 0)),
                pl.BlockSpec((panel, width), lambda i, *_: (0, 0)),
            ],
            scratch_shapes=[pltpu.VMEM((devices * cap, width), jnp.float32)],
        ),
        out_shape=[
            jax.ShapeDtypeStruct((total, width), jnp.float32),
            jax.ShapeDtypeStruct((panel, width), jnp.float32),
        ],
        cost_estimate=pl.CostEstimate(flops=0, transcendentals=0, bytes_accessed=16 * total * width),
        name="unpack",
    )(flags, at, *pieces)


def product_kernel(left_ref, right_ref, o_ref):
    o_ref[...] = dot3(*split(left_ref[...]), *split(right_ref[...]))


def product(left, right):
    rows, depth = left.shape
    width = right.shape[1]
    tile = math.gcd(rows, 32)
    return pl.pallas_call(
        product_kernel,
        grid=(rows // tile,),
        in_specs=[pl.BlockSpec((tile, depth), lambda i: (i, 0)), pl.BlockSpec((depth, width), lambda i: (0, 0))],
        out_specs=pl.BlockSpec((tile, width), lambda i: (i, 0)),
        out_shape=jax.ShapeDtypeStruct((rows, width), jnp.float32),
        name="product",
    )(left, right)


def select_kernel(place_ref, lower_ref, upper_ref, s_high, s_low, pick_ref, v_high, v_low, a_high, a_low, b_high, b_low):
    panel, depth = pick_ref.shape
    slots = lax.broadcasted_iota(jnp.int32, (1, depth), 1)
    chosen = jnp.where(place_ref[...] == slots, 1.0, 0.0).astype(jnp.bfloat16)
    pick_ref[...] = chosen[panel:]
    for target, side in zip((s_high, s_low), split(lower_ref[0])):
        target[...] = jnp.dot(side, chosen[:panel], preferred_element_type=jnp.float32).astype(jnp.bfloat16)
    v_high[...], v_low[...] = split(lower_ref[1])
    a_high[...], a_low[...] = split(upper_ref[0])
    b_high[...], b_low[...] = split(upper_ref[1])


def select(column, lower_inv, upper_inv, depth):
    panel = lower_inv.shape[1]
    shapes = [(panel, depth)] * 3 + [(panel, panel)] * 6
    return pl.pallas_call(
        select_kernel,
        in_specs=[pl.BlockSpec(memory_space=pltpu.VMEM)] * 3,
        out_shape=[jax.ShapeDtypeStruct(shape, jnp.bfloat16) for shape in shapes],
        name="select",
    )(column, lower_inv, upper_inv)


def corner_kernel(flag_ref, *refs):
    sent_ref, cross_ref, home_ref, swap_ref, lower_ref, a_high, a_low, top_ref, tail_ref = refs[:9]
    t_high, t_low, c_high, c_low, front_ref, low_full, up_full = refs[9:]
    at_home = flag_ref[3] > 0
    even = flag_ref[4] > 0
    mine = jnp.where(at_home, sent_ref[...], cross_ref[...])
    other = jnp.where(at_home, home_ref[...], swap_ref[...])
    low_full[...] = dot3(*split(jnp.where(even, mine, other)), a_high[...], a_low[...])
    up_full[...] = dot3(*split(lower_ref[0]), *split(jnp.where(even, other, mine)))
    t_high[...], t_low[...] = split(low_full[...])
    c_high[...], c_low[...] = split(up_full[...])
    part = top_ref.shape[0]
    start = pl.multiple_of(flag_ref[0] * part, 8)
    own_low = low_full[pl.ds(start, part), :]
    own_up = up_full[pl.ds(start, part), :]
    tail = tail_ref[...] - dot3(*split(own_low), c_high[...], c_low[...])
    first = flag_ref[2] == 0
    front_ref[0] = jnp.where(first, top_ref[...], own_up)
    front_ref[1] = jnp.where(first, own_low, tail)


def corner(flags, sent, moved, lower_inv, upper_parts, head, part):
    panel, width = sent.shape
    whole = lambda i, *_: (0, 0)
    square = pl.BlockSpec((panel, panel), whole)
    in_specs = [square] * 4 + [pl.BlockSpec((1, panel, panel), lambda i, *_: (0, 0, 0)), square, square]
    in_specs += [
        pl.BlockSpec((part, width), lambda i, flag: (flag[0], 0)),
        pl.BlockSpec((part, width), lambda i, flag: (panel // part + flag[0], 0)),
    ]
    return pl.pallas_call(
        corner_kernel,
        grid_spec=pltpu.PrefetchScalarGridSpec(
            num_scalar_prefetch=1,
            grid=(1,),
            in_specs=in_specs,
            out_specs=[square] * 4 + [pl.BlockSpec((2, part, width), lambda i, *_: (0, 0, 0))],
            scratch_shapes=[pltpu.VMEM((panel, panel), jnp.float32)] * 2,
        ),
        out_shape=[jax.ShapeDtypeStruct((panel, panel), jnp.bfloat16)] * 4
        + [jax.ShapeDtypeStruct((2, part, width), jnp.float32)],
        name="corner",
    )(flags, sent, *moved, lower_inv, *upper_parts, head, head)


def solve_kernel(flag_ref, at_ref, *refs, cap, widths, special):
    s_high, s_low, pick_ref, t_high, t_low, v_high, v_low, l_high, l_low, x_ref = refs[:10]
    pieces_count = (len(refs) - (19 if special else 18)) // len(widths)
    pieces = refs[10 : 10 + pieces_count * len(widths)]
    rest = refs[10 + pieces_count * len(widths) :]
    if special:
        alt_ref, rest = rest[0], rest[1:]
    u_high, u_low, front_ref, send_ref, g_high, g_low, u_full, y_ref = rest
    me = flag_ref[0]
    panel = pick_ref.shape[0]

    def put(row, col, value):
        high, low = split(value)
        g_high[row : row + value.shape[0], col : col + value.shape[1]] = high
        g_low[row : row + value.shape[0], col : col + value.shape[1]] = low

    offset = 0
    for chunk, per in enumerate(widths):
        index = pl.program_id(0) - offset

        @pl.when((index >= 0) & (index < per))
        def _():
            group = pieces[chunk * pieces_count : (chunk + 1) * pieces_count]
            load_pieces(group, cap, g_high.shape[1], index, per // 2, put)

        offset += per
    upper = dot3(s_high[...], s_low[...], g_high[...], g_low[...])
    u_full[:panel] = upper
    high, low = split(upper)
    u_high[0, :panel] = high
    u_low[0, :panel] = low
    picked = jnp.dot(pick_ref[...], g_high[...], preferred_element_type=jnp.float32)
    picked += jnp.dot(pick_ref[...], g_low[...], preferred_element_type=jnp.float32)
    reduced = picked - dot3(t_high[...], t_low[...], high, low)
    upper = dot3(v_high[...], v_low[...], *split(reduced))
    u_full[panel:] = upper
    high, low = split(upper)
    u_high[0, panel:] = high
    u_low[0, panel:] = low
    _, panels, part, width = front_ref.shape
    for index in range(panels):
        front_ref[0, index] = u_full[pl.ds(pl.multiple_of(index * panel + me * part, 8), part), :]
    old = x_ref[...].reshape(panels * part, width) - dot3(l_high[...], l_low[...], u_high[0], u_low[0])
    if special:
        old = jnp.where((flag_ref[1] > 0) & (pl.program_id(0) == 0), alt_ref[...], old)
    y_ref[...] = old
    devices, _, pair_cap, _ = send_ref.shape
    for target in range(devices):

        def load(row):
            return y_ref[pl.ds(at_ref[target * pair_cap + row], 1), :]

        def store(row, value):
            send_ref[target, 0, pl.ds(row, 1), :] = value

        move_rows(pair_cap, 8, load, store)


def solve(flags, at, factors, low, x, col, groups, alt, cap, devices, pair_cap, panels):
    panel, depth = factors[0].shape
    total = panels * panel
    _, _, part, width = x.shape
    widths = [pieces[0].shape[0] for pieces in groups]
    per = sum(widths)
    whole = lambda i, *_: (0, 0)
    in_specs = [pl.BlockSpec(factor.shape, whole) for factor in factors]
    in_specs += [
        pl.BlockSpec((panels * part, total), whole),
        pl.BlockSpec((panels * part, total), whole),
        pl.BlockSpec((panels, 1, part, width), lambda i, *_: (0, col + i, 0, 0)),
    ]
    args = [*factors, *low, x]
    for chunk, pieces in enumerate(groups):
        in_specs += piece_specs(pieces, sum(widths[:chunk]))
        args += pieces
    if alt is not None:
        in_specs.append(pl.BlockSpec((panels * part, width), whole))
        args.append(alt)
    return pl.pallas_call(
        functools.partial(solve_kernel, cap=cap, widths=widths, special=alt is not None),
        grid_spec=pltpu.PrefetchScalarGridSpec(
            num_scalar_prefetch=2,
            grid=(per,),
            in_specs=in_specs,
            out_specs=[
                pl.BlockSpec((1, total, width), lambda i, *_: (i, 0, 0)),
                pl.BlockSpec((1, total, width), lambda i, *_: (i, 0, 0)),
                pl.BlockSpec((1, panels, part, width), lambda i, *_: (i, 0, 0, 0)),
                pl.BlockSpec((devices, 1, pair_cap, width), lambda i, *_: (0, i, 0, 0)),
            ],
            scratch_shapes=[
                pltpu.VMEM((depth, width), jnp.bfloat16),
                pltpu.VMEM((depth, width), jnp.bfloat16),
                pltpu.VMEM((total, width), jnp.float32),
                pltpu.VMEM((panels * part, width), jnp.float32),
            ],
        ),
        out_shape=[
            jax.ShapeDtypeStruct((per, total, width), jnp.bfloat16),
            jax.ShapeDtypeStruct((per, total, width), jnp.bfloat16),
            jax.ShapeDtypeStruct((per, panels, part, width), jnp.float32),
            jax.ShapeDtypeStruct((devices, per, pair_cap, width), jnp.float32),
        ],
        cost_estimate=pl.CostEstimate(
            flops=6 * per * total * (depth + panels * part) * width,
            transcendentals=0,
            bytes_accessed=16 * per * total * width,
        ),
        name="solve",
    )(flags, at, *args)


def lower_kernel(flag_ref, *refs, first, panels):
    x_ref, cross_ref, home_ref, swap_ref, a_high, a_low, b_high, b_low, c_high, c_low = refs[:10]
    rest = refs[10:] if first else refs[13:]
    high_ref, low_ref, alt_ref = rest[:3]
    group, _, part, width = x_ref.shape
    at_home = flag_ref[3] > 0
    even = flag_ref[4] > 0
    mine = jnp.where(at_home, x_ref[...].reshape(group * part, width), cross_ref[...])
    other = jnp.where(at_home, home_ref[...], swap_ref[...])
    left = dot3(*split(jnp.where(even, mine, other)), a_high[...], a_low[...])
    left_parts = split(left)
    right = jnp.where(even, other, mine) - dot3(*left_parts, c_high[...], c_low[...])
    right = dot3(*split(right), b_high[...], b_low[...])
    right_parts = split(right)
    panel = left.shape[1]
    high_ref[:, :panel], low_ref[:, :panel] = left_parts
    high_ref[:, panel:], low_ref[:, panel:] = right_parts
    alt_ref[...] = jnp.where(flag_ref[2] == 0, left, right)
    if first:
        old_high, old_low, old_alt = rest[3:]

        @pl.when(pl.program_id(0) == 0)
        def _():
            count = panels * part
            old_high[...] = high_ref[:count]
            old_low[...] = low_ref[:count]
            old_alt[...] = alt_ref[:count]


def lower(flags, x, band, bands, moved, factors, previous):
    blocks, _, part, width = x.shape
    panel = factors[0].shape[0]
    panels = 2
    size = blocks // bands
    group = max(g for g in range(1, size + 1) if size % g == 0 and (g * part <= 256 or g == 1))
    group = max(group, panels) if size % panels == 0 and band == 0 else group
    steps = size // group
    offset = band * steps
    whole = lambda j, *_: (0, 0)
    in_specs = [pl.BlockSpec((group, 1, part, width), lambda j, *_: (offset + j, 0, 0, 0))]
    in_specs += [pl.BlockSpec((group * part, width), lambda j, *_: (j, 0))] * 3
    in_specs += [pl.BlockSpec(factor.shape, whole) for factor in factors]
    args = [x, *moved, *factors]
    out_specs = [
        pl.BlockSpec((group * part, panels * panel), lambda j, *_: (offset + j, 0)),
        pl.BlockSpec((group * part, panels * panel), lambda j, *_: (offset + j, 0)),
        pl.BlockSpec((group * part, width), lambda j, *_: (offset + j, 0)),
    ]
    out_shape = [
        jax.ShapeDtypeStruct((blocks * part, panels * panel), jnp.bfloat16),
        jax.ShapeDtypeStruct((blocks * part, panels * panel), jnp.bfloat16),
        jax.ShapeDtypeStruct((blocks * part, width), jnp.float32),
    ]
    aliases = {}
    if previous is None:
        old = panels * part
        for shape, kind in (
            ((old, panels * panel), jnp.bfloat16),
            ((old, panels * panel), jnp.bfloat16),
            ((old, width), jnp.float32),
        ):
            out_specs.append(pl.BlockSpec(shape, whole))
            out_shape.append(jax.ShapeDtypeStruct(shape, kind))
    else:
        in_specs += [pl.BlockSpec(memory_space=pl.ANY)] * 3
        aliases = {1 + len(args) + index: index for index in range(3)}
        args += previous
    return pl.pallas_call(
        functools.partial(lower_kernel, first=previous is None, panels=panels),
        grid_spec=pltpu.PrefetchScalarGridSpec(
            num_scalar_prefetch=1, grid=(steps,), in_specs=in_specs, out_specs=out_specs
        ),
        out_shape=out_shape,
        input_output_aliases=aliases,
        cost_estimate=pl.CostEstimate(
            flops=18 * size * part * panel * panel, transcendentals=0, bytes_accessed=28 * size * part * width
        ),
        name="lower",
    )(flags, *args)


def trail_kernel(flag_ref, row_ref, slot_ref, count_ref, *refs, special):
    x_ref, l_high, l_low, u_high, u_low, front_ref, come_ref = refs[:7]
    rest = refs[7:]
    if special:
        alt_ref, corner_ref, rest = rest[0], rest[1], rest[2:]
    o_ref = rest[-1]
    group, _, part, width = x_ref.shape
    band = pl.program_id(0)
    value = x_ref[...].reshape(group * part, width) - dot3(l_high[...], l_low[...], u_high[0], u_low[0])
    if special:
        chosen = (flag_ref[1] > 0) & (pl.program_id(1) == 0)
        value = jnp.where(chosen, alt_ref[...], value)
    o_ref[:, 0] = value.reshape(group, part, width)

    @pl.when(band == 0)
    def _():
        for index in range(front_ref.shape[1]):
            front = front_ref[0, index]
            if special:
                front = jnp.where(chosen, corner_ref[index], front)
            o_ref[index, 0] = front

    devices, _, pair_cap, _ = come_ref.shape
    base = band * (devices * pair_cap)

    def body(index, _):
        spot = row_ref[base + index]
        slot = slot_ref[base + index]
        o_ref[spot // part, 0, pl.ds(spot % part, 1), :] = come_ref[slot // pair_cap, 0, pl.ds(slot % pair_cap, 1), :]
        return 0

    lax.fori_loop(0, count_ref[band], body, 0)


def trail(flags, tables, x, col, low, upper, front, come, special, previous, bands):
    blocks, _, part, width = x.shape
    per, total, _ = upper[0].shape
    group = blocks // bands
    in_specs = [
        pl.BlockSpec((group, 1, part, width), lambda j, i, *_: (j, col + i, 0, 0)),
        pl.BlockSpec((group * part, total), lambda j, i, *_: (j, 0)),
        pl.BlockSpec((group * part, total), lambda j, i, *_: (j, 0)),
        pl.BlockSpec((1, total, width), lambda j, i, *_: (i, 0, 0)),
        pl.BlockSpec((1, total, width), lambda j, i, *_: (i, 0, 0)),
        pl.BlockSpec((1,) + front.shape[1:], lambda j, i, *_: (i, 0, 0, 0)),
        pl.BlockSpec((come.shape[0], 1) + come.shape[2:], lambda j, i, *_: (0, i, 0, 0)),
    ]
    args = [x, *low, *upper, front, come]
    if special is not None:
        alt, corner = special
        in_specs.append(pl.BlockSpec((group * part, width), lambda j, i, *_: (j, 0)))
        in_specs.append(pl.BlockSpec(corner.shape, lambda j, i, *_: (0, 0, 0)))
        args += [alt, corner]
    aliases = {}
    if previous is not None:
        in_specs.append(pl.BlockSpec(memory_space=pl.ANY))
        args.append(previous)
        aliases = {4 + len(args) - 1: 0}
    return pl.pallas_call(
        functools.partial(trail_kernel, special=special is not None),
        grid_spec=pltpu.PrefetchScalarGridSpec(
            num_scalar_prefetch=4,
            grid=(bands, per),
            in_specs=in_specs,
            out_specs=pl.BlockSpec((group, 1, part, width), lambda j, i, *_: (j, col + i, 0, 0)),
        ),
        out_shape=jax.ShapeDtypeStruct(x.shape, jnp.float32),
        input_output_aliases=aliases,
        cost_estimate=pl.CostEstimate(
            flops=6 * per * blocks * part * total * width,
            transcendentals=0,
            bytes_accessed=16 * per * blocks * part * width,
        ),
        name="trail",
    )(flags, *tables, *args)


def ring_gather(own, devices):
    order = list(range(0, devices, 2)) + list(range(devices - 1, 0, -2))
    forward = [(order[i], order[(i + 1) % devices]) for i in range(devices)]
    backward = [(b, a) for a, b in forward]
    ahead = behind = own
    ahead_list, behind_list = [], []
    for _ in range(devices // 2 - 1):
        ahead = lax.ppermute(ahead, "prow", forward)
        behind = lax.ppermute(behind, "prow", backward)
        ahead_list.append(ahead)
        behind_list.append(behind)
    if own.shape[0] % 2 == 0:
        half = own.shape[0] // 2
        left, right = ahead[:half], behind[half:]
    else:
        half = own.shape[2] // 2
        left, right = ahead[:, :, :half], behind[:, :, half:]
    left = lax.ppermute(left, "prow", forward)
    right = lax.ppermute(right, "prow", backward)
    return [own, *ahead_list, *reversed(behind_list), left, right]


def row_moves(block, col_index, col_devices):
    moving = crossed = block
    for hop in range(1, col_devices // 2):
        moving = lax.ppermute(moving, "pcol", [(2 * hop - 2, 2 * hop), (2 * hop - 1, 2 * hop + 1)])
        crossed = moving if hop == 1 else jnp.where(col_index // 2 == hop, moving, crossed)
    home = lax.ppermute(block, "pcol", [(0, 1), (1, 0)])
    rest = [(i, i ^ 1) for i in range(2, col_devices)]
    if not rest:
        return crossed, home, home
    swap = lax.ppermute(crossed, "pcol", rest)
    return crossed, home, swap


def panel_pair(block, col_index, col_devices):
    crossed, home, swap = row_moves(block, col_index, col_devices)
    at_home = col_index < 2
    mine = jnp.where(at_home, block, crossed)
    other = jnp.where(at_home, home, swap)
    even = col_index % 2 == 0
    return jnp.where(even, mine, other), jnp.where(even, other, mine)


def chunking(cols):
    if cols < 4:
        return [1] * cols
    middle = cols // 2
    return [1, middle, cols - 1 - middle]


def grouping(chunks):
    return [[chunk] for chunk in range(chunks)]


def fast(x, place, column, tables, lower_inv, upper_inv, sizes):
    panel, part, devices, cap, pair_cap, bands, rows = sizes
    send_at, out_at, in_tables = tables
    blocks, cols, _, width = x.shape
    panels = lower_inv.shape[0]
    row_index = lax.axis_index("prow")
    col_index = lax.axis_index("pcol")
    col_devices = lax.axis_size("pcol")
    widths = chunking(cols)
    chunks = [(sum(widths[:i]), per) for i, per in enumerate(widths)]
    flags = jnp.stack([row_index, col_index < panels, col_index, col_index < 2, col_index % 2 == 0]).astype(jnp.int32)
    raw = []
    for band in range(bands):
        block = x[band * (blocks // bands) : (band + 1) * (blocks // bands), 0].reshape(rows, width)
        raw.append(row_moves(block, col_index, col_devices))
    gathered = []
    for col, per in chunks:
        own = pack(send_at, x, col, per, cap)
        gathered.append(ring_gather(own, devices))
    head, sent = unpack(flags, place, gathered[0], cap, devices, panel)
    parts = select(column, lower_inv, upper_inv, devices * cap)
    s_high, s_low, pick, v_high, v_low = parts[:5]
    upper_parts = parts[5:]
    moved = row_moves(sent, col_index, col_devices)
    t_high, t_low, c_high, c_low, front_corner = corner(flags, sent, moved, lower_inv, upper_parts[:2], head, part)
    low = old = None
    for band in range(bands):
        outs = lower(flags, x, band, bands, raw[band], [*upper_parts, c_high, c_low], low)
        low = outs[:3]
        old = outs[3:] if band == 0 else old
    alt = low[2]
    factors = [s_high, s_low, pick, t_high, t_low, v_high, v_low]
    result = None
    for group in grouping(len(chunks)):
        col = chunks[group[0]][0]
        u_high, u_low, front, send = solve(
            flags,
            out_at,
            factors,
            old[:2],
            x,
            col,
            [gathered[chunk] for chunk in group],
            old[2] if col == 0 else None,
            cap,
            devices,
            pair_cap,
            panels,
        )
        come = lax.all_to_all(send, "prow", 0, 0, tiled=True)
        special = (alt, front_corner) if col == 0 else None
        result = trail(flags, in_tables, x, col, low[:2], (u_high, u_low), front, come, special, result, bands)
    return result


def slow(x, wanted, came_from, pivots, lower_inv, upper_inv, result, sizes):
    panel, part, devices = sizes[:3]
    blocks, cols, _, width = x.shape
    total = wanted.shape[0]
    x = plain(x)
    row_index = lax.axis_index("prow")
    col_index = lax.axis_index("pcol")
    col_devices = lax.axis_size("pcol")
    rows = jnp.arange(blocks, dtype=jnp.int32)[:, None] * panel + jnp.arange(part, dtype=jnp.int32)[None, :]
    rows = (rows + row_index * part).reshape(-1)
    spots = jnp.where(came_from >= 0, pivots, blocks * panel)
    source = jnp.full((blocks * panel,), -1, jnp.int32).at[spots].set(came_from, mode="drop")[rows]
    needed = jnp.concatenate([wanted, jnp.arange(total, dtype=jnp.int32)])
    mine = (needed % panel // part == row_index)[:, None]
    spot = needed // panel * part + needed % part
    around = [(i, (i + 1) % devices) for i in range(devices)]

    def swapped(col):
        here = lax.dynamic_index_in_dim(x, col, 1, False).reshape(blocks * part, width)
        moving = jnp.where(mine, here[spot], 0.0)

        def hop(_, carry):
            moving, gathered = carry
            moving = lax.ppermute(moving, "prow", around)
            return moving, gathered + moving

        _, gathered = lax.fori_loop(0, devices - 1, hop, (moving, moving))
        head = gathered[:total]
        return head, jnp.where((source >= 0)[:, None], gathered[total:][jnp.maximum(source, 0)], here)

    head, body = swapped(0)
    raw = panel_pair(body, col_index, col_devices)
    corner = panel_pair(head, col_index, col_devices)
    low_top = product(corner[0][panel:], upper_inv[0])
    up_side = product(lower_inv[0], corner[1][:panel])
    low_first = product(raw[0], upper_inv[0])
    low_second = product(raw[1] - product(low_first, up_side), upper_inv[1])

    def column(col, result):
        head, body = swapped(col)
        upper = product(lower_inv[0], head[:panel])
        reduced = head[panel:] - product(low_top, upper)
        second = product(lower_inv[1], reduced)
        body = body - product(low_first, upper) - product(low_second, second)
        left = (col == 0) & (col_index == 0)
        right = (col == 0) & (col_index == 1)
        body = jnp.where(left, low_first, jnp.where(right, low_second, body))
        upper = jnp.where(left, head[:panel], upper)
        second = jnp.where(left, low_top, jnp.where(right, reduced, second))
        own = [lax.dynamic_slice_in_dim(side, row_index * part, part, 0) for side in (upper, second)]
        body = jnp.concatenate([*own, body[2 * part :]], axis=0)
        return plain(lax.dynamic_update_index_in_dim(plain(result), body.reshape(blocks, part, width), col, 1))

    return lax.fori_loop(0, cols, column, result)


def local(matrix, pivots, lower_inv, upper_inv):
    row_blocks, row_part, _, _ = matrix.shape
    panels, panel = pivots.shape
    devices = lax.axis_size("prow")
    total = panels * panel
    mean = total / devices
    cap = -(-int(mean + 2.75 * math.sqrt(mean)) // 8) * 8
    pair_mean = mean / devices
    pair_cap = -(-int(pair_mean + 4 * math.sqrt(pair_mean)) // 8) * 8
    bands = 2 if row_blocks % 2 == 0 else 1
    sizes = (panel, row_part, devices, cap, pair_cap, bands, row_blocks // bands * row_part)
    x = matrix.transpose(0, 2, 1, 3)
    me = lax.axis_index("prow").astype(jnp.int32).reshape(1)
    send_at, place, column, out_at, in_rows, in_slots, counts, over, wanted, came_from = routing(me, pivots, sizes)
    tables = (send_at[0], out_at[0], (in_rows[0], in_slots[0], counts[0]))
    result = fast(x, place[0], column, tables, lower_inv, upper_inv, sizes)

    def again(carry):
        _, result = carry
        result = slow(x, wanted[0], came_from[0], pivots.reshape(-1), lower_inv, upper_inv, result, sizes)
        return jnp.int32(-1), plain(result)

    _, result = lax.while_loop(lambda carry: carry[0] >= 0, again, (over[0, 0], plain(result)))
    return result.transpose(0, 2, 1, 3)


def solution(mesh):
    return jax.shard_map(
        local,
        mesh=mesh,
        in_specs=(P(None, "prow", None, "pcol"), P(), P(), P()),
        out_specs=P(None, "prow", None, "pcol"),
        check_vma=False,
    )
```

profile of v0, /device:TPU:0, one launch (start us, length us, event | category | flops | bytes accessed | tf_op | source)
XLA Modules:
  0.0 412.0 jit_solution(8922980870423541218)
XLA Ops:
  1.7 9.9 %routing.1 = (s32[1,256]{1,0:T(1,128)}, s32[1,1024]{1,0:T(1,128)}, s32[1024,1]{1,0:T(8,128)}, s32[1,256]{1,0:T(1,128)}, s32[1,512]{1,0:T(1,128)}, /*index=5*/s32...) custom-call(s32[1]{0:T(128)} %bitcast.16.me_ref, ...), custom_call_target="tpu_custom_call" | custom-call | tf_op jit(solution)/shard_map/routing/pallas_call | solution.py:144
  11.6 8.2 %pack.5.refs_10_ = f32[3,160,512]{2,1,0:T(8,128)} custom-call(s32[256]{0:T(256)} %bitcast.100, f32[24,6,64,512]{3,2,1,0:T(8,128)} %bitcast.69), custom_call_target="tpu_custom_call" | custom-call | bytes 28311552 | tf_op jit(solution)/shard_map/pack/pallas_call | solution.py:180
  37.7 8.1 %collective-permute-done.36.refs_16_ = f32[3,160,512]{2,1,0:T(8,128)} collective-permute-done((f32[3,160,512]{2,1,0:T(8,128)}, f32[3,160,512]{2,1,0:T(8,128)}, u32[]{:S(2)}, u32[]{:S(2)}) %collective-permute-start.36) | collective-permute-done | bytes 983072 | tf_op jit(solution)/shard_map/ppermute | solution.py:625
  47.8 5.0 %collective-permute-done.14.refs_6_.refs_16_ = f32[1,160,512]{2,1,0:T(8,128)S(1)} collective-permute-done((f32[1,160,512]{2,1,0:T(8,128)}, f32[1,160,512]{2,1,0:T(8,128)S(1)}, u32[]{:S(2)}, u32[]{:S(2)}) %collective-permute-start.14) | collective-permute-done | bytes 327712 | tf_op jit(solution)/shard_map/ppermute | solution.py:625
  54.9 25.1 %collective-permute-done.15.refs_5_.refs_15_ = f32[1,160,512]{2,1,0:T(8,128)S(1)} collective-permute-done((f32[1,160,512]{2,1,0:T(8,128)S(1)}, f32[1,160,512]{2,1,0:T(8,128)S(1)}, u32[]{:S(2)}, u32[]{:S(2)}) %collective-permute-start.15) | collective-permute-done | bytes 327712 | tf_op jit(solution)/shard_map/ppermute | solution.py:625
  82.0 6.8 %collective-permute-done.16.refs_4_.refs_14_ = f32[1,160,512]{2,1,0:T(8,128)S(1)} collective-permute-done((f32[1,160,512]{2,1,0:T(8,128)S(1)}, f32[1,160,512]{2,1,0:T(8,128)S(1)}, u32[]{:S(2)}, u32[]{:S(2)}) %collective-permute-start.16) | collective-permute-done | bytes 327712 | tf_op jit(solution)/shard_map/ppermute | solution.py:625
  97.4 7.9 %unpack.1 = (f32[1024,512]{1,0:T(8,128)}, f32[512,512]{1,0:T(8,128)}) custom-call(s32[5]{0:T(128)} %stack.25.flag_ref, s32[1024]{0:T(1024)} %bitcast.106, f32[1,160,512]{2,1,0:T(8,128)} %pack.3.refs_0_.refs_10_, f32[1,160,512]{2,1,0:T(8,128)} %copy-done.17, f32[1,160,512]{2,1,0:T(8,128)} %copy-done.19, f32[1,160,512]{2,1,0:T(8,128)} %copy-done.14, ...), custom_call_target="tpu_custom_call" | custom-call | bytes 8388608 | tf_op jit(solution)/shard_map/unpack/pallas_call | solution.py:240
  114.6 14.9 %collective-permute-done.34.refs_12_ = f32[3,160,512]{2,1,0:T(8,128)} collective-permute-done((f32[3,160,512]{2,1,0:T(8,128)}, f32[3,160,512]{2,1,0:T(8,128)}, u32[]{:S(2)}, u32[]{:S(2)}) %collective-permute-start.34) | collective-permute-done | bytes 983072 | tf_op jit(solution)/shard_map/ppermute | solution.py:624
  133.6 6.3 %pack.4.refs_10_ = f32[2,160,512]{2,1,0:T(8,128)} custom-call(s32[256]{0:T(256)} %bitcast.102, f32[24,6,64,512]{3,2,1,0:T(8,128)} %bitcast.72), custom_call_target="tpu_custom_call" | custom-call | bytes 18874368 | tf_op jit(solution)/shard_map/pack/pallas_call | solution.py:180
  139.9 7.3 %select.84 = (bf16[512,1280]{1,0:T(8,128)(2,1)}, bf16[512,1280]{1,0:T(8,128)(2,1)}, bf16[512,1280]{1,0:T(8,128)(2,1)}, bf16[512,512]{1,0:T(8,128)(2,1)}, bf16[51...) custom-call(s32[1024,1]{1,0:T(8,128)} %get-tuple-element.440.place_r, ...), custom_call_target="tpu_custom_call" | custom-call | tf_op jit(solution)/shard_map/select/pallas_call | solution.py:294
  148.3 9.5 %collective-permute-done.35.refs_13_ = f32[3,160,512]{2,1,0:T(8,128)} collective-permute-done((f32[3,160,512]{2,1,0:T(8,128)}, f32[3,160,512]{2,1,0:T(8,128)}, u32[]{:S(2)}, u32[]{:S(2)}) %collective-permute-start.35) | collective-permute-done | bytes 983072 | tf_op jit(solution)/shard_map/ppermute | solution.py:624
  161.7 6.8 %corner.1 = (bf16[512,512]{1,0:T(8,128)(2,1)}, bf16[512,512]{1,0:T(8,128)(2,1)}, bf16[512,512]{1,0:T(8,128)(2,1)}, bf16[512,512]{1,0:T(8,128)(2,1)}, f32[2,64,512]{2,1,0:T(8,128)}) custom-call(s32[5]{0:T(128)} %stack.25.flag_ref, f32[512,512]{1,0:T(8,128)} %get-tuple-element.447.refs_0_, f32[512,512]{1,0:T(8,128)} %copy-done.20, ...), custom_call_target="tpu_custom_call" | custom-call | tf_op jit(solution)/shard_map/corner/pallas_call | solution.py:332
  170.6 9.9 %lower.2 = (bf16[1536,1024]{1,0:T(8,128)(2,1)}, bf16[1536,1024]{1,0:T(8,128)(2,1)}, f32[1536,512]{1,0:T(8,128)}, bf16[128,1024]{1,0:T(8,128)(2,1)}, bf16[128,1024]{1,0:T(8,128)(2,1)}, /*index=5*/f32[128,512]{1,0:T(8,128)}) custom-call(s32[5]{0:T(128)} %stack.25.flag_ref, f32[24,6,64,512]{3,2,1,0:T(8,128)} %bitcast.73, f32[768,512]{1,0:T(8,128)} %copy-done.15, ...), custom_call_target="tpu_custom_call" | custom-call | flops 3623878656 | bytes 11010048 | tf_op jit(solution)/shard_map/lower/pallas_call | solution.py:526
  180.5 12.8 %solve.5 = (bf16[1,1024,512]{2,1,0:T(8,128)(2,1)}, bf16[1,1024,512]{2,1,0:T(8,128)(2,1)}, f32[1,2,64,512]{3,2,1,0:T(8,128)}, f32[8,1,32,512]{3,2,1,0:T(8,128)}) custom-call(s32[5]{0:T(128)} %stack.25.flag_ref, s32[256]{0:T(256)} %bitcast.107, bf16[512,1280]{1,0:T(8,128)(2,1)} %get-tuple-element.457.refs_0_, bf16[512,1280]{1,0:T(8,128)(2,1)} %get-tuple-element.458.refs_1_, ...), custom_call_target="tpu_custom_call" | custom-call | flops 4429185024 | bytes 8388608 | tf_op jit(solution)/shard_map/solve/pallas_call | solution.py:425
  201.6 27.9 %solve.4 = (bf16[3,1024,512]{2,1,0:T(8,128)(2,1)}, bf16[3,1024,512]{2,1,0:T(8,128)(2,1)}, f32[3,2,64,512]{3,2,1,0:T(8,128)}, f32[8,3,32,512]{3,2,1,0:T(8,128)}) custom-call(s32[5]{0:T(128)} %stack.25.flag_ref, s32[256]{0:T(256)} %bitcast.108, bf16[512,1280]{1,0:T(8,128)(2,1)} %get-tuple-element.457.refs_0_, bf16[512,1280]{1,0:T(8,128)(2,1)} %get-tuple-element.458.refs_1_, ...), custom_call_target="tpu_custom_call" | custom-call | flops 13287555072 | bytes 25165824 | tf_op jit(solution)/shard_map/solve/pallas_call | solution.py:425
  229.5 6.0 %all-to-all-start.1 = ((f32[8,3,32,512]{3,2,1,0:T(8,128)}), f32[8,3,32,512]{3,2,1,0:T(8,128)S(1)}, u32[]{:S(2)}, u32[]{:S(2)}) async-start(f32[8,3,32,512]{3,2,1,0:T(8,128)} %get-tuple-element.473), calls=%async_computation.1 | async-start | bytes 3145728 | tf_op jit(solution)/shard_map/all_to_all | solution.py:721
  237.6 37.5 %collective-permute-done.29.refs_15_ = f32[2,160,512]{2,1,0:T(8,128)S(1)} collective-permute-done((f32[2,160,512]{2,1,0:T(8,128)}, f32[2,160,512]{2,1,0:T(8,128)S(1)}, u32[]{:S(2)}, u32[]{:S(2)}) %collective-permute-start.29) | collective-permute-done | bytes 655392 | tf_op jit(solution)/shard_map/ppermute | solution.py:625
  275.1 10.6 %collective-permute-start.27 = (f32[2,160,512]{2,1,0:T(8,128)S(1)}, f32[2,160,512]{2,1,0:T(8,128)S(1)}, u32[]{:S(2)}, u32[]{:S(2)}) collective-permute-start(f32[2,160,512]{2,1,0:T(8,128)S(1)} %collective-permute-done.26.refs_12_), channel_id=1, source_target_pairs={{0,8},{8,16},{16,24},{24,28},{28,20},{20,12},{12,4},{4,0},{1,9},{9... | collective-permute-start | bytes 1966088 | tf_op jit(solution)/shard_map/ppermute | solution.py:624
  289.4 8.5 %collective-permute-done.30.refs_14_ = f32[2,160,512]{2,1,0:T(8,128)S(1)} collective-permute-done((f32[2,160,512]{2,1,0:T(8,128)S(1)}, f32[2,160,512]{2,1,0:T(8,128)S(1)}, u32[]{:S(2)}, u32[]{:S(2)}) %collective-permute-start.30) | collective-permute-done | bytes 655392 | tf_op jit(solution)/shard_map/ppermute | solution.py:625
  308.9 20.7 %solve.3 = (bf16[2,1024,512]{2,1,0:T(8,128)(2,1)}, bf16[2,1024,512]{2,1,0:T(8,128)(2,1)}, f32[2,2,64,512]{3,2,1,0:T(8,128)}, f32[8,2,32,512]{3,2,1,0:T(8,128)}) custom-call(s32[5]{0:T(128)} %stack.25.flag_ref, s32[256]{0:T(256)} %bitcast.109, bf16[512,1280]{1,0:T(8,128)(2,1)} %get-tuple-element.457.refs_0_, bf16[512,1280]{1,0:T(8,128)(2,1)} %get-tuple-element.458.refs_1_, ...), custom_call_target="tpu_custom_call" | custom-call | flops 8858370048 | bytes 16777216 | tf_op jit(solution)/shard_map/solve/pallas_call | solution.py:425
  334.4 9.7 %lower.3 = (bf16[1536,1024]{1,0:T(8,128)(2,1)}, bf16[1536,1024]{1,0:T(8,128)(2,1)}, f32[1536,512]{1,0:T(8,128)}) custom-call(s32[5]{0:T(128)} %stack.25.flag_ref, f32[24,6,64,512]{3,2,1,0:T(8,128)} %bitcast.77, f32[768,512]{1,0:T(8,128)} %collective-permute-done.8.refs_1_, ...), custom_call_target="tpu_custom_call", output_to_operand_aliasing={{0}: (11, {}), {1}: (12, {}), {2}: (13, {})} | custom-call | flops 3623878656 | bytes 11010048 | tf_op jit(solution)/shard_map/lower/pallas_call | solution.py:526
  344.1 14.4 %trail.3.refs_7_ = f32[24,6,64,512]{3,2,1,0:T(8,128)} custom-call(s32[5]{0:T(128)} %stack.25.flag_ref, s32[512]{0:T(512)} %bitcast.94, s32[512]{0:T(512)} %bitcast.97, s32[128]{0:T(128)} %bitcast.103, f32[24,6,64,512]{3,2,1,0:T(8,128)} %bitcast.78, bf16[1536,1024]{1,0:T(8,128)(2,1)} %get-tuple-element.454.refs_1_, ...), custom_call_target="tpu_custom_call" | custom-call | flops 4831838208 | bytes 12582912 | tf_op jit(solution)/shard_map/trail/pallas_call | solution.py:598
  358.5 29.8 %trail.4.refs_7_ = f32[24,6,64,512]{3,2,1,0:T(8,128)} custom-call(s32[5]{0:T(128)} %stack.25.flag_ref, s32[512]{0:T(512)} %bitcast.95, s32[512]{0:T(512)} %bitcast.98, s32[128]{0:T(128)} %bitcast.104, f32[24,6,64,512]{3,2,1,0:T(8,128)} %bitcast.79, bf16[1536,1024]{1,0:T(8,128)(2,1)} %get-tuple-element.454.refs_1_, ...), custom_call_target="tpu_custom_call", output_to_operand_aliasing={{}: (11, {})} | custom-call | flops 14495514624 | bytes 37748736 | tf_op jit(solution)/shard_map/trail/pallas_call | solution.py:598
  389.4 21.5 %trail.5 = f32[24,6,64,512]{3,2,1,0:T(8,128)} custom-call(s32[5]{0:T(128)} %stack.25.flag_ref, s32[512]{0:T(512)} %bitcast.96, s32[512]{0:T(512)} %bitcast.99, s32[128]{0:T(128)} %bitcast.105, f32[24,6,64,512]{3,2,1,0:T(8,128)} %bitcast.80, bf16[1536,1024]{1,0:T(8,128)(2,1)} %get-tuple-element.454.refs_1_, ...), custom_call_target="tpu_custom_call", output_to_operand_aliasing={{}: (11, {})} | custom-call | flops 9663676416 | bytes 25165824 | tf_op jit(solution)/shard_map/trail/pallas_call | solution.py:598
  (108 shorter events, 86.0 us)
Async XLA Ops:
  19.9 26.0 %collective-permute-start.36 = (f32[3,160,512]{2,1,0:T(8,128)}, f32[3,160,512]{2,1,0:T(8,128)}, u32[]{:S(2)}, u32[]{:S(2)}) collective-permute-start(f32[3,160,512]{2,1,0:T(8,128)} %pack.5.refs_10_), channel_id=1, source_target_pairs={{8,0},{16,8},{24,16},{28,24},{20,28},{12,20},{4,12},{0,4},{9,1},{1... | collective-permute-start | bytes 2949128 | tf_op jit(solution)/shard_map/ppermute | solution.py:625
  29.1 25.6 %collective-permute-start.11 = (f32[1,160,512]{2,1,0:T(8,128)}, f32[1,160,512]{2,1,0:T(8,128)S(1)}, u32[]{:S(2)}, u32[]{:S(2)}) collective-permute-start(f32[1,160,512]{2,1,0:T(8,128)} %pack.3.refs_0_.refs_10_), channel_id=1, source_target_pairs={{0,8},{8,16},{16,24},{24,28},{28,20},{20,12},{12,4},{4,0},{1,9},{9... | collective-permute-start | bytes 983048 | tf_op jit(solution)/shard_map/ppermute | solution.py:624
  33.6 79.2 %collective-permute-start.22 = (f32[768,512]{1,0:T(8,128)}, f32[768,512]{1,0:T(8,128)S(1)}, u32[]{:S(2)}, u32[]{:S(2)}) collective-permute-start(f32[768,512]{1,0:T(8,128)} %bitcast.28), channel_id=1, source_target_pairs={{0,2},{1,3},{4,6},{5,7},{8,10},{9,11},{12,14},{13,15},{16,18},{17,... | collective-permute-start | bytes 4718600 | tf_op jit(solution)/shard_map/ppermute | solution.py:642
  37.2 71.7 %collective-permute-start.33 = (f32[3,160,512]{2,1,0:T(8,128)}, f32[3,160,512]{2,1,0:T(8,128)}, u32[]{:S(2)}, u32[]{:S(2)}) collective-permute-start(f32[3,160,512]{2,1,0:T(8,128)} %pack.5.refs_10_), channel_id=1, source_target_pairs={{0,8},{8,16},{16,24},{24,28},{28,20},{20,12},{12,4},{4,0},{1,9},{9... | collective-permute-start | bytes 2949128 | tf_op jit(solution)/shard_map/ppermute | solution.py:624
  45.8 63.6 %collective-permute-start.37 = (f32[3,160,512]{2,1,0:T(8,128)}, f32[3,160,512]{2,1,0:T(8,128)}, u32[]{:S(2)}, u32[]{:S(2)}) collective-permute-start(f32[3,160,512]{2,1,0:T(8,128)} %collective-permute-done.36.refs_16_), channel_id=1, source_target_pairs={{8,0},{16,8},{24,16},{28,24},{20,28},{12,20},{4,12},{0,4},{9,1},{1... | collective-permute-start | bytes 2949128 | tf_op jit(solution)/shard_map/ppermute | solution.py:625
  52.8 27.2 %collective-permute-start.15 = (f32[1,160,512]{2,1,0:T(8,128)S(1)}, f32[1,160,512]{2,1,0:T(8,128)S(1)}, u32[]{:S(2)}, u32[]{:S(2)}) collective-permute-start(f32[1,160,512]{2,1,0:T(8,128)S(1)} %collective-permute-done.14.refs_6_.refs_16_), channel_id=1, source_target_pairs={{8,0},{16,8},{24,16},{28,24},{20,28},{12,20},{4,12},{0,4},{9,1},{1... | collective-permute-start | bytes 983048 | tf_op jit(solution)/shard_map/ppermute | solution.py:625
  54.7 27.0 %collective-permute-start.12 = (f32[1,160,512]{2,1,0:T(8,128)S(1)}, f32[1,160,512]{2,1,0:T(8,128)S(1)}, u32[]{:S(2)}, u32[]{:S(2)}) collective-permute-start(f32[1,160,512]{2,1,0:T(8,128)S(1)} %collective-permute-done.11.refs_1_.refs_11_), channel_id=1, source_target_pairs={{0,8},{8,16},{16,24},{24,28},{28,20},{20,12},{12,4},{4,0},{1,9},{9... | collective-permute-start | bytes 983048 | tf_op jit(solution)/shard_map/ppermute | solution.py:624
  105.3 26.2 %collective-permute-start.19 = (f32[512,512]{1,0:T(8,128)}, f32[512,512]{1,0:T(8,128)S(1)}, u32[]{:S(2)}, u32[]{:S(2)}) collective-permute-start(f32[512,512]{1,0:T(8,128)} %get-tuple-element.447.refs_0_), channel_id=1, source_target_pairs={{0,2},{1,3},{4,6},{5,7},{8,10},{9,11},{12,14},{13,15},{16,18},{17,... | collective-permute-start | bytes 3145736 | tf_op jit(solution)/shard_map/ppermute | solution.py:642
  110.9 59.2 %collective-permute-start.23 = (f32[768,512]{1,0:T(8,128)}, f32[768,512]{1,0:T(8,128)}, u32[]{:S(2)}, u32[]{:S(2)}) collective-permute-start(f32[768,512]{1,0:T(8,128)} %bitcast.28), channel_id=1, source_target_pairs={{0,1},{1,0},{4,5},{5,4},{8,9},{9,8},{12,13},{13,12},{16,17},{17,16... | collective-permute-start | bytes 4718600 | tf_op jit(solution)/shard_map/ppermute | solution.py:644
  112.8 57.7 %collective-permute-start.24 = (f32[768,512]{1,0:T(8,128)S(1)}, f32[768,512]{1,0:T(8,128)}, u32[]{:S(2)}, u32[]{:S(2)}) collective-permute-start(f32[768,512]{1,0:T(8,128)S(1)} %collective-permute-done.22.refs_1_), channel_id=1, source_target_pairs={{2,3},{3,2},{6,7},{7,6},{10,11},{11,10},{14,15},{15,14},{18,19},{1... | collective-permute-start | bytes 4718600 | tf_op jit(solution)/shard_map/ppermute | solution.py:648
  129.6 31.7 %collective-permute-start.20 = (f32[512,512]{1,0:T(8,128)}, f32[512,512]{1,0:T(8,128)}, u32[]{:S(2)}, u32[]{:S(2)}) collective-permute-start(f32[512,512]{1,0:T(8,128)} %get-tuple-element.447.refs_0_), channel_id=1, source_target_pairs={{0,1},{1,0},{4,5},{5,4},{8,9},{9,8},{12,13},{13,12},{16,17},{17,16... | collective-permute-start | bytes 3145736 | tf_op jit(solution)/shard_map/ppermute | solution.py:644
  131.5 30.2 %collective-permute-start.21 = (f32[512,512]{1,0:T(8,128)S(1)}, f32[512,512]{1,0:T(8,128)}, u32[]{:S(2)}, u32[]{:S(2)}) collective-permute-start(f32[512,512]{1,0:T(8,128)S(1)} %collective-permute-done.19.refs_1_), channel_id=1, source_target_pairs={{2,3},{3,2},{6,7},{7,6},{10,11},{11,10},{14,15},{15,14},{18,19},{1... | collective-permute-start | bytes 3145736 | tf_op jit(solution)/shard_map/ppermute | solution.py:648
  159.7 75.8 %collective-permute-start.28 = (f32[2,160,512]{2,1,0:T(8,128)}, f32[2,160,512]{2,1,0:T(8,128)}, u32[]{:S(2)}, u32[]{:S(2)}) collective-permute-start(f32[2,160,512]{2,1,0:T(8,128)} %pack.4.refs_10_), channel_id=1, source_target_pairs={{8,0},{16,8},{24,16},{28,24},{20,28},{12,20},{4,12},{0,4},{9,1},{1... | collective-permute-start | bytes 1966088 | tf_op jit(solution)/shard_map/ppermute | solution.py:625
  161.3 76.2 %collective-permute-start.25 = (f32[2,160,512]{2,1,0:T(8,128)}, f32[2,160,512]{2,1,0:T(8,128)}, u32[]{:S(2)}, u32[]{:S(2)}) collective-permute-start(f32[2,160,512]{2,1,0:T(8,128)} %pack.4.refs_10_), channel_id=1, source_target_pairs={{0,8},{8,16},{16,24},{24,28},{28,20},{20,12},{12,4},{4,0},{1,9},{9... | collective-permute-start | bytes 1966088 | tf_op jit(solution)/shard_map/ppermute | solution.py:624
  168.5 33.0 %collective-permute-start.40 = (f32[3,160,256]{2,1,0:T(8,128)S(1)}, f32[3,160,256]{2,1,0:T(8,128)}, u32[]{:S(2)}, u32[]{:S(2)}) collective-permute-start(f32[3,160,256]{2,1,0:T(8,128)S(1)} %slice.141), channel_id=1, source_target_pairs={{8,0},{16,8},{24,16},{28,24},{20,28},{12,20},{4,12},{0,4},{9,1},{1... | collective-permute-start | bytes 1474568 | tf_op jit(solution)/shard_map/ppermute | solution.py:635
  170.1 31.4 %collective-permute-start.39 = (f32[3,160,256]{2,1,0:T(8,128)}, f32[3,160,256]{2,1,0:T(8,128)}, u32[]{:S(2)}, u32[]{:S(2)}) collective-permute-start(f32[3,160,256]{2,1,0:T(8,128)} %slice.140), channel_id=1, source_target_pairs={{0,8},{8,16},{16,24},{24,28},{28,20},{20,12},{12,4},{4,0},{1,9},{9... | collective-permute-start | bytes 1474568 | tf_op jit(solution)/shard_map/ppermute | solution.py:634
  193.3 36.1 %all-to-all-start.2 = ((f32[8,1,32,512]{3,2,1,0:T(8,128)}), f32[8,1,32,512]{3,2,1,0:T(8,128)S(1)}, u32[]{:S(2)}, u32[]{:S(2)}) async-start(f32[8,1,32,512]{3,2,1,0:T(8,128)} %get-tuple-element.478), calls=%async_computation.2 | async-start | bytes 1048576 | tf_op jit(solution)/shard_map/all_to_all | solution.py:721
  198.2 89.4 %collective-permute-start.8 = (f32[768,512]{1,0:T(8,128)}, f32[768,512]{1,0:T(8,128)}, u32[]{:S(2)}, u32[]{:S(2)}) collective-permute-start(f32[768,512]{1,0:T(8,128)} %bitcast.25), channel_id=1, source_target_pairs={{0,2},{1,3},{4,6},{5,7},{8,10},{9,11},{12,14},{13,15},{16,18},{17,... | collective-permute-start | bytes 4718600 | tf_op jit(solution)/shard_map/ppermute | solution.py:642
  229.5 100.1 %all-to-all-start.1 = ((f32[8,3,32,512]{3,2,1,0:T(8,128)}), f32[8,3,32,512]{3,2,1,0:T(8,128)S(1)}, u32[]{:S(2)}, u32[]{:S(2)}) async-start(f32[8,3,32,512]{3,2,1,0:T(8,128)} %get-tuple-element.473), calls=%async_computation.1 | async-start | bytes 3145728 | tf_op jit(solution)/shard_map/all_to_all | solution.py:721
  235.5 39.6 %collective-permute-start.29 = (f32[2,160,512]{2,1,0:T(8,128)}, f32[2,160,512]{2,1,0:T(8,128)S(1)}, u32[]{:S(2)}, u32[]{:S(2)}) collective-permute-start(f32[2,160,512]{2,1,0:T(8,128)} %collective-permute-done.28.refs_16_), channel_id=1, source_target_pairs={{8,0},{16,8},{24,16},{28,24},{20,28},{12,20},{4,12},{0,4},{9,1},{1... | collective-permute-start | bytes 1966088 | tf_op jit(solution)/shard_map/ppermute | solution.py:625
  237.5 37.5 %collective-permute-start.26 = (f32[2,160,512]{2,1,0:T(8,128)}, f32[2,160,512]{2,1,0:T(8,128)S(1)}, u32[]{:S(2)}, u32[]{:S(2)}) collective-permute-start(f32[2,160,512]{2,1,0:T(8,128)} %collective-permute-done.25.refs_11_), channel_id=1, source_target_pairs={{0,8},{8,16},{16,24},{24,28},{28,20},{20,12},{12,4},{4,0},{1,9},{9... | collective-permute-start | bytes 1966088 | tf_op jit(solution)/shard_map/ppermute | solution.py:624
  285.6 48.8 %collective-permute-start.9 = (f32[768,512]{1,0:T(8,128)}, f32[768,512]{1,0:T(8,128)}, u32[]{:S(2)}, u32[]{:S(2)}) collective-permute-start(f32[768,512]{1,0:T(8,128)} %bitcast.25), channel_id=1, source_target_pairs={{0,1},{1,0},{4,5},{5,4},{8,9},{9,8},{12,13},{13,12},{16,17},{17,16... | collective-permute-start | bytes 4718600 | tf_op jit(solution)/shard_map/ppermute | solution.py:644
  287.6 46.9 %collective-permute-start.10 = (f32[768,512]{1,0:T(8,128)}, f32[768,512]{1,0:T(8,128)}, u32[]{:S(2)}, u32[]{:S(2)}) collective-permute-start(f32[768,512]{1,0:T(8,128)} %collective-permute-done.8.refs_1_), channel_id=1, source_target_pairs={{2,3},{3,2},{6,7},{7,6},{10,11},{11,10},{14,15},{15,14},{18,19},{1... | collective-permute-start | bytes 4718600 | tf_op jit(solution)/shard_map/ppermute | solution.py:648
  329.6 58.7 %all-to-all-start = ((f32[8,2,32,512]{3,2,1,0:T(8,128)}), f32[8,2,32,512]{3,2,1,0:T(8,128)S(1)}, u32[]{:S(2)}, u32[]{:S(2)}) async-start(f32[8,2,32,512]{3,2,1,0:T(8,128)} %get-tuple-element.469), calls=%async_computation | async-start | bytes 2097152 | tf_op jit(solution)/shard_map/all_to_all | solution.py:721
  (29 other events, 538.3 us)
where the time goes:
time: 420 us; the launch traced here: 412 us
  Pallas kernels  198 us (47%)
  waiting for transfers between devices  128 us (30%)
  starting transfers between devices  72.2 us (17%)
  local copies, waits for them, and re-layouts  12.8 us (3%)
    ppermute x9, waiting for transfers between devices, ring_gather(): behind = lax.ppermute(behind, 'prow', backward)  91.1 us
    pallas_call x3, Pallas kernels, trail(): pl.pallas_call(functools.partial(trail_kernel, special=special is not Non...  65.8 us
    pallas_call x3, Pallas kernels, solve(): pl.pallas_call(functools.partial(solve_kernel, cap=cap, widths=widths, sp...  61.4 us
    ppermute x9, waiting for transfers between devices, ring_gather(): ahead = lax.ppermute(ahead, 'prow', forward)  24.8 us
    pallas_call x2, Pallas kernels, lower(): pl.pallas_call(functools.partial(lower_kernel, first=previous is None, pa...  19.6 us
    pallas_call x3, Pallas kernels, pack(): pl.pallas_call(functools.partial(pack_kernel, part=part), grid_spec=pltpu...  19.3 us
    all_to_all x3, starting transfers between devices, fast(): come = lax.all_to_all(send, 'prow', 0, 0, tiled=True)  15.7 us
    ppermute x9, starting transfers between devices, ring_gather(): behind = lax.ppermute(behind, 'prow', backward)  15.2 us
  transfers between devices with their start and end apart: 36, of which 13 were waited for; matrix products, arithmetic and copies ran while one was open for 2% of the time, Pallas kernels for 38%

commit v1 on v0

--- a/solution.py
+++ b/solution.py
@@ -44,8 +44,7 @@
 
 def routing_kernel(
     me_ref,
-    piv_row,
-    piv_col,
+    piv_ref,
     send_ref,
     place_ref,
     column_ref,
@@ -60,10 +59,10 @@
     sizes,
 ):
     panel, part, devices, cap, pair_cap, _, rows = sizes
-    total = piv_row.shape[1]
+    total = piv_ref.shape[0] * piv_ref.shape[1]
     me = me_ref[0]
-    p_row = piv_row[...]
-    p_col = piv_col[...]
+    p_row = jnp.concatenate([piv_ref[index : index + 1, :] for index in range(piv_ref.shape[0])], axis=1)
+    p_col = turned(p_row)
     lane = lax.broadcasted_iota(jnp.int32, (1, total), 1)
     sub = lax.broadcasted_iota(jnp.int32, (total, 1), 0)
 
@@ -147,10 +146,9 @@
         in_specs=[
             pl.BlockSpec(memory_space=pltpu.SMEM),
             pl.BlockSpec(memory_space=pltpu.VMEM),
-            pl.BlockSpec(memory_space=pltpu.VMEM),
         ],
         name="routing",
-    )(me, pivots.reshape(1, total), pivots.reshape(total, 1))
+    )(me, pivots)
 
 
 def move_rows(count, unroll, load, store):

time: 420 us -> 418 us (level)
  transfers between devices with their start and end apart: 36 -> 36, of which waited for: 13 -> 13; matrix products, arithmetic and copies ran while one was open for 2% -> 2% of each run, Pallas kernels for 38% -> 39%
where the time goes in v1:
time: 418 us; the launch traced here: 410 us
  Pallas kernels  198 us (47%)
  waiting for transfers between devices  128 us (31%)
  starting transfers between devices  72.2 us (17%)
  local copies, waits for them, and re-layouts  10.9 us (3%)
    ppermute x9, waiting for transfers between devices, ring_gather(): behind = lax.ppermute(behind, 'prow', backward)  91.1 us
    pallas_call x3, Pallas kernels, trail(): pl.pallas_call(functools.partial(trail_kernel, special=special is not Non...  65.7 us
    pallas_call x3, Pallas kernels, solve(): pl.pallas_call(functools.partial(solve_kernel, cap=cap, widths=widths, sp...  61.3 us
    ppermute x9, waiting for transfers between devices, ring_gather(): ahead = lax.ppermute(ahead, 'prow', forward)  24.8 us
    pallas_call x2, Pallas kernels, lower(): pl.pallas_call(functools.partial(lower_kernel, first=previous is None, pa...  19.6 us
    pallas_call x3, Pallas kernels, pack(): pl.pallas_call(functools.partial(pack_kernel, part=part), grid_spec=pltpu...  19.3 us
    all_to_all x3, starting transfers between devices, fast(): come = lax.all_to_all(send, 'prow', 0, 0, tiled=True)  15.7 us
    ppermute x9, starting transfers between devices, ring_gather(): behind = lax.ppermute(behind, 'prow', backward)  15.2 us
  transfers between devices with their start and end apart: 36, of which 13 were waited for; matrix products, arithmetic and copies ran while one was open for 2% of the time, Pallas kernels for 39%

profile of v1, /device:TPU:0, one launch (start us, length us, event | category | flops | bytes accessed | tf_op | source)
XLA Modules:
  0.0 410.0 jit_solution(5965328349838632534)
XLA Ops:
  0.0 9.7 %routing.1 = (s32[1,256]{1,0:T(1,128)}, s32[1,1024]{1,0:T(1,128)}, s32[1024,1]{1,0:T(8,128)}, s32[1,256]{1,0:T(1,128)}, s32[1,512]{1,0:T(1,128)}, /*index=5*/s32...) custom-call(s32[1]{0:T(128)} %bitcast.16.me_ref, s32[2,512]{1,0:T(2,128)} %piv_ref.1), custom_call_target="tpu_custom_call" | custom-call | tf_op jit(solution)/shard_map/routing/pallas_call | solution.py:143
  9.7 8.2 %pack.5.refs_10_ = f32[3,160,512]{2,1,0:T(8,128)} custom-call(s32[256]{0:T(256)} %bitcast.90, f32[24,6,64,512]{3,2,1,0:T(8,128)} %bitcast.62), custom_call_target="tpu_custom_call" | custom-call | bytes 28311552 | tf_op jit(solution)/shard_map/pack/pallas_call | solution.py:178
  35.8 8.1 %collective-permute-done.36.refs_16_ = f32[3,160,512]{2,1,0:T(8,128)} collective-permute-done((f32[3,160,512]{2,1,0:T(8,128)}, f32[3,160,512]{2,1,0:T(8,128)}, u32[]{:S(2)}, u32[]{:S(2)}) %collective-permute-start.36) | collective-permute-done | bytes 983072 | tf_op jit(solution)/shard_map/ppermute | solution.py:623
  45.9 5.0 %collective-permute-done.14.refs_6_.refs_16_ = f32[1,160,512]{2,1,0:T(8,128)S(1)} collective-permute-done((f32[1,160,512]{2,1,0:T(8,128)}, f32[1,160,512]{2,1,0:T(8,128)S(1)}, u32[]{:S(2)}, u32[]{:S(2)}) %collective-permute-start.14) | collective-permute-done | bytes 327712 | tf_op jit(solution)/shard_map/ppermute | solution.py:623
  53.0 25.1 %collective-permute-done.15.refs_5_.refs_15_ = f32[1,160,512]{2,1,0:T(8,128)S(1)} collective-permute-done((f32[1,160,512]{2,1,0:T(8,128)S(1)}, f32[1,160,512]{2,1,0:T(8,128)S(1)}, u32[]{:S(2)}, u32[]{:S(2)}) %collective-permute-start.15) | collective-permute-done | bytes 327712 | tf_op jit(solution)/shard_map/ppermute | solution.py:623
  80.1 6.8 %collective-permute-done.16.refs_4_.refs_14_ = f32[1,160,512]{2,1,0:T(8,128)S(1)} collective-permute-done((f32[1,160,512]{2,1,0:T(8,128)S(1)}, f32[1,160,512]{2,1,0:T(8,128)S(1)}, u32[]{:S(2)}, u32[]{:S(2)}) %collective-permute-start.16) | collective-permute-done | bytes 327712 | tf_op jit(solution)/shard_map/ppermute | solution.py:623
  95.5 7.9 %unpack.1 = (f32[1024,512]{1,0:T(8,128)}, f32[512,512]{1,0:T(8,128)}) custom-call(s32[5]{0:T(128)} %stack.25.flag_ref, s32[1024]{0:T(1024)} %bitcast.96, f32[1,160,512]{2,1,0:T(8,128)} %pack.3.refs_0_.refs_10_, f32[1,160,512]{2,1,0:T(8,128)} %copy-done.17, f32[1,160,512]{2,1,0:T(8,128)} %copy-done.19, f32[1,160,512]{2,1,0:T(8,128)} %copy-done.14, ...), custom_call_target="tpu_custom_call" | custom-call | bytes 8388608 | tf_op jit(solution)/shard_map/unpack/pallas_call | solution.py:238
  112.7 14.9 %collective-permute-done.34.refs_12_ = f32[3,160,512]{2,1,0:T(8,128)} collective-permute-done((f32[3,160,512]{2,1,0:T(8,128)}, f32[3,160,512]{2,1,0:T(8,128)}, u32[]{:S(2)}, u32[]{:S(2)}) %collective-permute-start.34) | collective-permute-done | bytes 983072 | tf_op jit(solution)/shard_map/ppermute | solution.py:622
  131.7 6.3 %pack.4.refs_10_ = f32[2,160,512]{2,1,0:T(8,128)} custom-call(s32[256]{0:T(256)} %bitcast.92, f32[24,6,64,512]{3,2,1,0:T(8,128)} %bitcast.65), custom_call_target="tpu_custom_call" | custom-call | bytes 18874368 | tf_op jit(solution)/shard_map/pack/pallas_call | solution.py:178
  138.0 7.3 %select.84 = (bf16[512,1280]{1,0:T(8,128)(2,1)}, bf16[512,1280]{1,0:T(8,128)(2,1)}, bf16[512,1280]{1,0:T(8,128)(2,1)}, bf16[512,512]{1,0:T(8,128)(2,1)}, bf16[51...) custom-call(s32[1024,1]{1,0:T(8,128)} %get-tuple-element.440.place_r, ...), custom_call_target="tpu_custom_call" | custom-call | tf_op jit(solution)/shard_map/select/pallas_call | solution.py:292
  146.4 9.5 %collective-permute-done.35.refs_13_ = f32[3,160,512]{2,1,0:T(8,128)} collective-permute-done((f32[3,160,512]{2,1,0:T(8,128)}, f32[3,160,512]{2,1,0:T(8,128)}, u32[]{:S(2)}, u32[]{:S(2)}) %collective-permute-start.35) | collective-permute-done | bytes 983072 | tf_op jit(solution)/shard_map/ppermute | solution.py:622
  159.8 6.8 %corner.1 = (bf16[512,512]{1,0:T(8,128)(2,1)}, bf16[512,512]{1,0:T(8,128)(2,1)}, bf16[512,512]{1,0:T(8,128)(2,1)}, bf16[512,512]{1,0:T(8,128)(2,1)}, f32[2,64,512]{2,1,0:T(8,128)}) custom-call(s32[5]{0:T(128)} %stack.25.flag_ref, f32[512,512]{1,0:T(8,128)} %get-tuple-element.447.refs_0_, f32[512,512]{1,0:T(8,128)} %copy-done.20, ...), custom_call_target="tpu_custom_call" | custom-call | tf_op jit(solution)/shard_map/corner/pallas_call | solution.py:330
  168.7 9.9 %lower.2 = (bf16[1536,1024]{1,0:T(8,128)(2,1)}, bf16[1536,1024]{1,0:T(8,128)(2,1)}, f32[1536,512]{1,0:T(8,128)}, bf16[128,1024]{1,0:T(8,128)(2,1)}, bf16[128,1024]{1,0:T(8,128)(2,1)}, /*index=5*/f32[128,512]{1,0:T(8,128)}) custom-call(s32[5]{0:T(128)} %stack.25.flag_ref, f32[24,6,64,512]{3,2,1,0:T(8,128)} %bitcast.66, f32[768,512]{1,0:T(8,128)} %copy-done.15, ...), custom_call_target="tpu_custom_call" | custom-call | flops 3623878656 | bytes 11010048 | tf_op jit(solution)/shard_map/lower/pallas_call | solution.py:524
  178.6 12.9 %solve.5 = (bf16[1,1024,512]{2,1,0:T(8,128)(2,1)}, bf16[1,1024,512]{2,1,0:T(8,128)(2,1)}, f32[1,2,64,512]{3,2,1,0:T(8,128)}, f32[8,1,32,512]{3,2,1,0:T(8,128)}) custom-call(s32[5]{0:T(128)} %stack.25.flag_ref, s32[256]{0:T(256)} %bitcast.97, bf16[512,1280]{1,0:T(8,128)(2,1)} %get-tuple-element.457.refs_0_, bf16[512,1280]{1,0:T(8,128)(2,1)} %get-tuple-element.458.refs_1_, ...), custom_call_target="tpu_custom_call" | custom-call | flops 4429185024 | bytes 8388608 | tf_op jit(solution)/shard_map/solve/pallas_call | solution.py:423
  199.7 27.9 %solve.4 = (bf16[3,1024,512]{2,1,0:T(8,128)(2,1)}, bf16[3,1024,512]{2,1,0:T(8,128)(2,1)}, f32[3,2,64,512]{3,2,1,0:T(8,128)}, f32[8,3,32,512]{3,2,1,0:T(8,128)}) custom-call(s32[5]{0:T(128)} %stack.25.flag_ref, s32[256]{0:T(256)} %bitcast.98, bf16[512,1280]{1,0:T(8,128)(2,1)} %get-tuple-element.457.refs_0_, bf16[512,1280]{1,0:T(8,128)(2,1)} %get-tuple-element.458.refs_1_, ...), custom_call_target="tpu_custom_call" | custom-call | flops 13287555072 | bytes 25165824 | tf_op jit(solution)/shard_map/solve/pallas_call | solution.py:423
  227.6 6.0 %all-to-all-start.1 = ((f32[8,3,32,512]{3,2,1,0:T(8,128)}), f32[8,3,32,512]{3,2,1,0:T(8,128)S(1)}, u32[]{:S(2)}, u32[]{:S(2)}) async-start(f32[8,3,32,512]{3,2,1,0:T(8,128)} %get-tuple-element.473), calls=%async_computation.1 | async-start | bytes 3145728 | tf_op jit(solution)/shard_map/all_to_all | solution.py:719
  235.7 37.5 %collective-permute-done.29.refs_15_ = f32[2,160,512]{2,1,0:T(8,128)S(1)} collective-permute-done((f32[2,160,512]{2,1,0:T(8,128)}, f32[2,160,512]{2,1,0:T(8,128)S(1)}, u32[]{:S(2)}, u32[]{:S(2)}) %collective-permute-start.29) | collective-permute-done | bytes 655392 | tf_op jit(solution)/shard_map/ppermute | solution.py:623
  273.2 10.6 %collective-permute-start.27 = (f32[2,160,512]{2,1,0:T(8,128)S(1)}, f32[2,160,512]{2,1,0:T(8,128)S(1)}, u32[]{:S(2)}, u32[]{:S(2)}) collective-permute-start(f32[2,160,512]{2,1,0:T(8,128)S(1)} %collective-permute-done.26.refs_12_), channel_id=1, source_target_pairs={{0,8},{8,16},{16,24},{24,28},{28,20},{20,12},{12,4},{4,0},{1,9},{9... | collective-permute-start | bytes 1966088 | tf_op jit(solution)/shard_map/ppermute | solution.py:622
  287.5 8.5 %collective-permute-done.30.refs_14_ = f32[2,160,512]{2,1,0:T(8,128)S(1)} collective-permute-done((f32[2,160,512]{2,1,0:T(8,128)S(1)}, f32[2,160,512]{2,1,0:T(8,128)S(1)}, u32[]{:S(2)}, u32[]{:S(2)}) %collective-permute-start.30) | collective-permute-done | bytes 655392 | tf_op jit(solution)/shard_map/ppermute | solution.py:623
  307.0 20.6 %solve.3 = (bf16[2,1024,512]{2,1,0:T(8,128)(2,1)}, bf16[2,1024,512]{2,1,0:T(8,128)(2,1)}, f32[2,2,64,512]{3,2,1,0:T(8,128)}, f32[8,2,32,512]{3,2,1,0:T(8,128)}) custom-call(s32[5]{0:T(128)} %stack.25.flag_ref, s32[256]{0:T(256)} %bitcast.99, bf16[512,1280]{1,0:T(8,128)(2,1)} %get-tuple-element.457.refs_0_, bf16[512,1280]{1,0:T(8,128)(2,1)} %get-tuple-element.458.refs_1_, ...), custom_call_target="tpu_custom_call" | custom-call | flops 8858370048 | bytes 16777216 | tf_op jit(solution)/shard_map/solve/pallas_call | solution.py:423
  332.5 9.7 %lower.3 = (bf16[1536,1024]{1,0:T(8,128)(2,1)}, bf16[1536,1024]{1,0:T(8,128)(2,1)}, f32[1536,512]{1,0:T(8,128)}) custom-call(s32[5]{0:T(128)} %stack.25.flag_ref, f32[24,6,64,512]{3,2,1,0:T(8,128)} %bitcast.70, f32[768,512]{1,0:T(8,128)} %collective-permute-done.8.refs_1_, ...), custom_call_target="tpu_custom_call", output_to_operand_aliasing={{0}: (11, {}), {1}: (12, {}), {2}: (13, {})} | custom-call | flops 3623878656 | bytes 11010048 | tf_op jit(solution)/shard_map/lower/pallas_call | solution.py:524
  342.1 14.3 %trail.3.refs_7_ = f32[24,6,64,512]{3,2,1,0:T(8,128)} custom-call(s32[5]{0:T(128)} %stack.25.flag_ref, s32[512]{0:T(512)} %bitcast.84, s32[512]{0:T(512)} %bitcast.87, s32[128]{0:T(128)} %bitcast.93, f32[24,6,64,512]{3,2,1,0:T(8,128)} %bitcast.71, bf16[1536,1024]{1,0:T(8,128)(2,1)} %get-tuple-element.454.refs_1_, ...), custom_call_target="tpu_custom_call" | custom-call | flops 4831838208 | bytes 12582912 | tf_op jit(solution)/shard_map/trail/pallas_call | solution.py:596
  356.5 29.8 %trail.4.refs_7_ = f32[24,6,64,512]{3,2,1,0:T(8,128)} custom-call(s32[5]{0:T(128)} %stack.25.flag_ref, s32[512]{0:T(512)} %bitcast.85, s32[512]{0:T(512)} %bitcast.88, s32[128]{0:T(128)} %bitcast.94, f32[24,6,64,512]{3,2,1,0:T(8,128)} %bitcast.72, bf16[1536,1024]{1,0:T(8,128)(2,1)} %get-tuple-element.454.refs_1_, ...), custom_call_target="tpu_custom_call", output_to_operand_aliasing={{}: (11, {})} | custom-call | flops 14495514624 | bytes 37748736 | tf_op jit(solution)/shard_map/trail/pallas_call | solution.py:596
  387.4 21.5 %trail.5 = f32[24,6,64,512]{3,2,1,0:T(8,128)} custom-call(s32[5]{0:T(128)} %stack.25.flag_ref, s32[512]{0:T(512)} %bitcast.86, s32[512]{0:T(512)} %bitcast.89, s32[128]{0:T(128)} %bitcast.95, f32[24,6,64,512]{3,2,1,0:T(8,128)} %bitcast.73, bf16[1536,1024]{1,0:T(8,128)(2,1)} %get-tuple-element.454.refs_1_, ...), custom_call_target="tpu_custom_call", output_to_operand_aliasing={{}: (11, {})} | custom-call | flops 9663676416 | bytes 25165824 | tf_op jit(solution)/shard_map/trail/pallas_call | solution.py:596
  (104 shorter events, 84.2 us)
Async XLA Ops:
  18.0 26.0 %collective-permute-start.36 = (f32[3,160,512]{2,1,0:T(8,128)}, f32[3,160,512]{2,1,0:T(8,128)}, u32[]{:S(2)}, u32[]{:S(2)}) collective-permute-start(f32[3,160,512]{2,1,0:T(8,128)} %pack.5.refs_10_), channel_id=1, source_target_pairs={{8,0},{16,8},{24,16},{28,24},{20,28},{12,20},{4,12},{0,4},{9,1},{1... | collective-permute-start | bytes 2949128 | tf_op jit(solution)/shard_map/ppermute | solution.py:623
  27.2 25.6 %collective-permute-start.11 = (f32[1,160,512]{2,1,0:T(8,128)}, f32[1,160,512]{2,1,0:T(8,128)S(1)}, u32[]{:S(2)}, u32[]{:S(2)}) collective-permute-start(f32[1,160,512]{2,1,0:T(8,128)} %pack.3.refs_0_.refs_10_), channel_id=1, source_target_pairs={{0,8},{8,16},{16,24},{24,28},{28,20},{20,12},{12,4},{4,0},{1,9},{9... | collective-permute-start | bytes 983048 | tf_op jit(solution)/shard_map/ppermute | solution.py:622
  31.7 79.2 %collective-permute-start.22 = (f32[768,512]{1,0:T(8,128)}, f32[768,512]{1,0:T(8,128)S(1)}, u32[]{:S(2)}, u32[]{:S(2)}) collective-permute-start(f32[768,512]{1,0:T(8,128)} %bitcast.28), channel_id=1, source_target_pairs={{0,2},{1,3},{4,6},{5,7},{8,10},{9,11},{12,14},{13,15},{16,18},{17,... | collective-permute-start | bytes 4718600 | tf_op jit(solution)/shard_map/ppermute | solution.py:640
  35.3 71.6 %collective-permute-start.33 = (f32[3,160,512]{2,1,0:T(8,128)}, f32[3,160,512]{2,1,0:T(8,128)}, u32[]{:S(2)}, u32[]{:S(2)}) collective-permute-start(f32[3,160,512]{2,1,0:T(8,128)} %pack.5.refs_10_), channel_id=1, source_target_pairs={{0,8},{8,16},{16,24},{24,28},{28,20},{20,12},{12,4},{4,0},{1,9},{9... | collective-permute-start | bytes 2949128 | tf_op jit(solution)/shard_map/ppermute | solution.py:622
  43.9 63.5 %collective-permute-start.37 = (f32[3,160,512]{2,1,0:T(8,128)}, f32[3,160,512]{2,1,0:T(8,128)}, u32[]{:S(2)}, u32[]{:S(2)}) collective-permute-start(f32[3,160,512]{2,1,0:T(8,128)} %collective-permute-done.36.refs_16_), channel_id=1, source_target_pairs={{8,0},{16,8},{24,16},{28,24},{20,28},{12,20},{4,12},{0,4},{9,1},{1... | collective-permute-start | bytes 2949128 | tf_op jit(solution)/shard_map/ppermute | solution.py:623
  50.9 27.2 %collective-permute-start.15 = (f32[1,160,512]{2,1,0:T(8,128)S(1)}, f32[1,160,512]{2,1,0:T(8,128)S(1)}, u32[]{:S(2)}, u32[]{:S(2)}) collective-permute-start(f32[1,160,512]{2,1,0:T(8,128)S(1)} %collective-permute-done.14.refs_6_.refs_16_), channel_id=1, source_target_pairs={{8,0},{16,8},{24,16},{28,24},{20,28},{12,20},{4,12},{0,4},{9,1},{1... | collective-permute-start | bytes 983048 | tf_op jit(solution)/shard_map/ppermute | solution.py:623
  52.8 27.0 %collective-permute-start.12 = (f32[1,160,512]{2,1,0:T(8,128)S(1)}, f32[1,160,512]{2,1,0:T(8,128)S(1)}, u32[]{:S(2)}, u32[]{:S(2)}) collective-permute-start(f32[1,160,512]{2,1,0:T(8,128)S(1)} %collective-permute-done.11.refs_1_.refs_11_), channel_id=1, source_target_pairs={{0,8},{8,16},{16,24},{24,28},{28,20},{20,12},{12,4},{4,0},{1,9},{9... | collective-permute-start | bytes 983048 | tf_op jit(solution)/shard_map/ppermute | solution.py:622
  103.4 26.2 %collective-permute-start.19 = (f32[512,512]{1,0:T(8,128)}, f32[512,512]{1,0:T(8,128)S(1)}, u32[]{:S(2)}, u32[]{:S(2)}) collective-permute-start(f32[512,512]{1,0:T(8,128)} %get-tuple-element.447.refs_0_), channel_id=1, source_target_pairs={{0,2},{1,3},{4,6},{5,7},{8,10},{9,11},{12,14},{13,15},{16,18},{17,... | collective-permute-start | bytes 3145736 | tf_op jit(solution)/shard_map/ppermute | solution.py:640
  109.0 59.2 %collective-permute-start.23 = (f32[768,512]{1,0:T(8,128)}, f32[768,512]{1,0:T(8,128)}, u32[]{:S(2)}, u32[]{:S(2)}) collective-permute-start(f32[768,512]{1,0:T(8,128)} %bitcast.28), channel_id=1, source_target_pairs={{0,1},{1,0},{4,5},{5,4},{8,9},{9,8},{12,13},{13,12},{16,17},{17,16... | collective-permute-start | bytes 4718600 | tf_op jit(solution)/shard_map/ppermute | solution.py:642
  110.9 57.7 %collective-permute-start.24 = (f32[768,512]{1,0:T(8,128)S(1)}, f32[768,512]{1,0:T(8,128)}, u32[]{:S(2)}, u32[]{:S(2)}) collective-permute-start(f32[768,512]{1,0:T(8,128)S(1)} %collective-permute-done.22.refs_1_), channel_id=1, source_target_pairs={{2,3},{3,2},{6,7},{7,6},{10,11},{11,10},{14,15},{15,14},{18,19},{1... | collective-permute-start | bytes 4718600 | tf_op jit(solution)/shard_map/ppermute | solution.py:646
  127.6 31.7 %collective-permute-start.20 = (f32[512,512]{1,0:T(8,128)}, f32[512,512]{1,0:T(8,128)}, u32[]{:S(2)}, u32[]{:S(2)}) collective-permute-start(f32[512,512]{1,0:T(8,128)} %get-tuple-element.447.refs_0_), channel_id=1, source_target_pairs={{0,1},{1,0},{4,5},{5,4},{8,9},{9,8},{12,13},{13,12},{16,17},{17,16... | collective-permute-start | bytes 3145736 | tf_op jit(solution)/shard_map/ppermute | solution.py:642
  129.6 30.2 %collective-permute-start.21 = (f32[512,512]{1,0:T(8,128)S(1)}, f32[512,512]{1,0:T(8,128)}, u32[]{:S(2)}, u32[]{:S(2)}) collective-permute-start(f32[512,512]{1,0:T(8,128)S(1)} %collective-permute-done.19.refs_1_), channel_id=1, source_target_pairs={{2,3},{3,2},{6,7},{7,6},{10,11},{11,10},{14,15},{15,14},{18,19},{1... | collective-permute-start | bytes 3145736 | tf_op jit(solution)/shard_map/ppermute | solution.py:646
  157.8 75.9 %collective-permute-start.28 = (f32[2,160,512]{2,1,0:T(8,128)}, f32[2,160,512]{2,1,0:T(8,128)}, u32[]{:S(2)}, u32[]{:S(2)}) collective-permute-start(f32[2,160,512]{2,1,0:T(8,128)} %pack.4.refs_10_), channel_id=1, source_target_pairs={{8,0},{16,8},{24,16},{28,24},{20,28},{12,20},{4,12},{0,4},{9,1},{1... | collective-permute-start | bytes 1966088 | tf_op jit(solution)/shard_map/ppermute | solution.py:623
  159.3 76.3 %collective-permute-start.25 = (f32[2,160,512]{2,1,0:T(8,128)}, f32[2,160,512]{2,1,0:T(8,128)}, u32[]{:S(2)}, u32[]{:S(2)}) collective-permute-start(f32[2,160,512]{2,1,0:T(8,128)} %pack.4.refs_10_), channel_id=1, source_target_pairs={{0,8},{8,16},{16,24},{24,28},{28,20},{20,12},{12,4},{4,0},{1,9},{9... | collective-permute-start | bytes 1966088 | tf_op jit(solution)/shard_map/ppermute | solution.py:622
  166.6 33.1 %collective-permute-start.40 = (f32[3,160,256]{2,1,0:T(8,128)S(1)}, f32[3,160,256]{2,1,0:T(8,128)}, u32[]{:S(2)}, u32[]{:S(2)}) collective-permute-start(f32[3,160,256]{2,1,0:T(8,128)S(1)} %slice.141), channel_id=1, source_target_pairs={{8,0},{16,8},{24,16},{28,24},{20,28},{12,20},{4,12},{0,4},{9,1},{1... | collective-permute-start | bytes 1474568 | tf_op jit(solution)/shard_map/ppermute | solution.py:633
  168.2 31.5 %collective-permute-start.39 = (f32[3,160,256]{2,1,0:T(8,128)}, f32[3,160,256]{2,1,0:T(8,128)}, u32[]{:S(2)}, u32[]{:S(2)}) collective-permute-start(f32[3,160,256]{2,1,0:T(8,128)} %slice.140), channel_id=1, source_target_pairs={{0,8},{8,16},{16,24},{24,28},{28,20},{20,12},{12,4},{4,0},{1,9},{9... | collective-permute-start | bytes 1474568 | tf_op jit(solution)/shard_map/ppermute | solution.py:632
  191.4 36.1 %all-to-all-start.2 = ((f32[8,1,32,512]{3,2,1,0:T(8,128)}), f32[8,1,32,512]{3,2,1,0:T(8,128)S(1)}, u32[]{:S(2)}, u32[]{:S(2)}) async-start(f32[8,1,32,512]{3,2,1,0:T(8,128)} %get-tuple-element.478), calls=%async_computation.2 | async-start | bytes 1048576 | tf_op jit(solution)/shard_map/all_to_all | solution.py:719
  196.3 89.4 %collective-permute-start.8 = (f32[768,512]{1,0:T(8,128)}, f32[768,512]{1,0:T(8,128)}, u32[]{:S(2)}, u32[]{:S(2)}) collective-permute-start(f32[768,512]{1,0:T(8,128)} %bitcast.25), channel_id=1, source_target_pairs={{0,2},{1,3},{4,6},{5,7},{8,10},{9,11},{12,14},{13,15},{16,18},{17,... | collective-permute-start | bytes 4718600 | tf_op jit(solution)/shard_map/ppermute | solution.py:640
  227.6 100.1 %all-to-all-start.1 = ((f32[8,3,32,512]{3,2,1,0:T(8,128)}), f32[8,3,32,512]{3,2,1,0:T(8,128)S(1)}, u32[]{:S(2)}, u32[]{:S(2)}) async-start(f32[8,3,32,512]{3,2,1,0:T(8,128)} %get-tuple-element.473), calls=%async_computation.1 | async-start | bytes 3145728 | tf_op jit(solution)/shard_map/all_to_all | solution.py:719
  233.6 39.5 %collective-permute-start.29 = (f32[2,160,512]{2,1,0:T(8,128)}, f32[2,160,512]{2,1,0:T(8,128)S(1)}, u32[]{:S(2)}, u32[]{:S(2)}) collective-permute-start(f32[2,160,512]{2,1,0:T(8,128)} %collective-permute-done.28.refs_16_), channel_id=1, source_target_pairs={{8,0},{16,8},{24,16},{28,24},{20,28},{12,20},{4,12},{0,4},{9,1},{1... | collective-permute-start | bytes 1966088 | tf_op jit(solution)/shard_map/ppermute | solution.py:623
  235.7 37.5 %collective-permute-start.26 = (f32[2,160,512]{2,1,0:T(8,128)}, f32[2,160,512]{2,1,0:T(8,128)S(1)}, u32[]{:S(2)}, u32[]{:S(2)}) collective-permute-start(f32[2,160,512]{2,1,0:T(8,128)} %collective-permute-done.25.refs_11_), channel_id=1, source_target_pairs={{0,8},{8,16},{16,24},{24,28},{28,20},{20,12},{12,4},{4,0},{1,9},{9... | collective-permute-start | bytes 1966088 | tf_op jit(solution)/shard_map/ppermute | solution.py:622
  283.8 48.7 %collective-permute-start.9 = (f32[768,512]{1,0:T(8,128)}, f32[768,512]{1,0:T(8,128)}, u32[]{:S(2)}, u32[]{:S(2)}) collective-permute-start(f32[768,512]{1,0:T(8,128)} %bitcast.25), channel_id=1, source_target_pairs={{0,1},{1,0},{4,5},{5,4},{8,9},{9,8},{12,13},{13,12},{16,17},{17,16... | collective-permute-start | bytes 4718600 | tf_op jit(solution)/shard_map/ppermute | solution.py:642
  285.7 46.8 %collective-permute-start.10 = (f32[768,512]{1,0:T(8,128)}, f32[768,512]{1,0:T(8,128)}, u32[]{:S(2)}, u32[]{:S(2)}) collective-permute-start(f32[768,512]{1,0:T(8,128)} %collective-permute-done.8.refs_1_), channel_id=1, source_target_pairs={{2,3},{3,2},{6,7},{7,6},{10,11},{11,10},{14,15},{15,14},{18,19},{1... | collective-permute-start | bytes 4718600 | tf_op jit(solution)/shard_map/ppermute | solution.py:646
  327.7 58.7 %all-to-all-start = ((f32[8,2,32,512]{3,2,1,0:T(8,128)}), f32[8,2,32,512]{3,2,1,0:T(8,128)S(1)}, u32[]{:S(2)}, u32[]{:S(2)}) async-start(f32[8,2,32,512]{3,2,1,0:T(8,128)} %get-tuple-element.469), calls=%async_computation | async-start | bytes 2097152 | tf_op jit(solution)/shard_map/all_to_all | solution.py:719
  (28 other events, 537.0 us)
